TPU v7x, 32 devices: a whole 2x2x4 slice. The times are simulated.
32 devices in a mesh: ctx: 8 (over z, x), head: 4 (over y, core).
Axes of the slice: x: 2, y: 2, z: 4, core: 2. Of those that a mesh axis runs over, the one named last changes fastest.
Arguments:
- hidden: bfloat16 [256, 8192], P(None, 'ctx')
- norm_gain: float32 [8192], replicated, may hold values from 0.1 to 1.9
- w_query: bfloat16 [8192, 8192], P('ctx', 'head'), may hold values from -0.0625 to 0.0625
- manifest_keys: bfloat16 [8, 4096, 128], P(None, 'ctx')
- manifest_values: bfloat16 [8, 4096, 128], P(None, 'ctx'), may hold values from -6 to 6
- w_output: bfloat16 [8192, 8192], P('head', 'ctx'), may hold values from -0.0625 to 0.0625
- valid_len: int32 [256], replicated, may hold values from 1 to 4096, as said below
- home_block: int32 [256], replicated, may hold values from 0 to 7, as said below
Outputs:
- projected: float32 [256, 8192], P('head', 'ctx')
Inputs may be any that keep to these rules, and one draw needn't show every extreme that they name: `valid_len`: every draw has a row that reads the whole manifest and a row with length 1. `home_block`: every draw assigns some row to the first block and some row to the last.
All inputs are finite; a program needn't handle non-finite values.
Results may differ from a plain program's by a relative error of at most 0.005.
The roundings to bfloat16 on the way count: a program that leaves them out, or rounds other values in their place, can miss the bound.
Values may be sent and summed in bfloat16 or wider, within the bound.
A program may use at most 128 MiB of HBM per device.

v0:
```python
import math
import jax
import jax.numpy as jnp
from jax import lax
from jax.sharding import PartitionSpec as P

H = 64
KVH = 8
HD = 128


def shards(
    hidden, norm_gain, w_query, manifest_keys, manifest_values, w_output, valid_len, home_block
):
    ctx_count = lax.axis_size("ctx")
    ctx_index = lax.axis_index("ctx")
    head_index = lax.axis_index("head")
    rows, feat = hidden.shape
    d_model = feat * ctx_count
    width = w_query.shape[1]
    heads_here = width // HD
    group = H // KVH
    span = manifest_keys.shape[1]
    hsplit = min(ctx_count, heads_here)
    rsplit = ctx_count // hsplit
    rows_dev = rows // rsplit
    heads_dev = heads_here // hsplit
    widened = hidden.astype(jnp.float32)
    total_sq = lax.psum(jnp.sum(widened * widened, axis=1, keepdims=True), "ctx")
    inv_rms = lax.rsqrt(total_sq / d_model + 1e-05)
    gain = lax.dynamic_slice_in_dim(norm_gain, ctx_index * feat, feat, 0)
    normed = (widened * inv_rms * gain[None, :]).astype(jnp.bfloat16)
    partial = jnp.dot(normed, w_query, preferred_element_type=jnp.float32)
    partial = partial.reshape(rsplit, rows_dev, hsplit, heads_dev * HD).transpose(2, 0, 1, 3)
    partial = partial.reshape(ctx_count, rows_dev, heads_dev * HD)
    query = lax.psum_scatter(partial, "ctx", scatter_dimension=0, tiled=False).astype(jnp.bfloat16)
    dest_heads = head_index * heads_here + jnp.arange(ctx_count) // rsplit * heads_dev
    dest_kv = dest_heads // group
    kv = jnp.stack([manifest_keys[dest_kv], manifest_values[dest_kv]], axis=1)
    kv = lax.all_to_all(kv, "ctx", split_axis=0, concat_axis=0, tiled=True)
    kv = kv.transpose(1, 0, 2, 3).reshape(2, ctx_count * span, HD)
    keys, values = (kv[0], kv[1])
    first_row = ctx_index % rsplit * rows_dev
    lens = lax.dynamic_slice_in_dim(valid_len, first_row, rows_dev, 0)
    blocks = lax.dynamic_slice_in_dim(home_block, first_row, rows_dev, 0)
    places = jnp.arange(ctx_count * span, dtype=jnp.int32)
    usable = (places[None, :] < lens[:, None]) | ((places // span)[None, :] == blocks[:, None])
    usable = usable[:, None, :]
    q3 = query.reshape(rows_dev, heads_dev, HD)
    scores = jnp.einsum("nhd,jd->nhj", q3, keys, preferred_element_type=jnp.float32) * (
        1.0 / math.sqrt(HD)
    )
    scores = jnp.where(usable, scores, -1e30)
    row_max = jnp.max(scores, axis=2, keepdims=True)
    expo = jnp.where(usable, jnp.exp(scores - row_max), 0.0)
    row_sum = jnp.sum(expo, axis=2, keepdims=True)
    weighted = jnp.einsum(
        "nhj,jd->nhd", expo.astype(jnp.bfloat16), values, preferred_element_type=jnp.float32
    )
    attn = (weighted / row_sum).astype(jnp.bfloat16).reshape(rows_dev, heads_dev * HD)
    attn = lax.all_gather(attn, "ctx", axis=0, tiled=False)
    attn = attn.reshape(hsplit, rsplit, rows_dev, heads_dev * HD).transpose(1, 2, 0, 3)
    attn = attn.reshape(rows, width)
    return lax.psum_scatter(
        jnp.dot(attn, w_output, preferred_element_type=jnp.float32),
        "head",
        scatter_dimension=0,
        tiled=True,
    )


def solution(mesh):
    in_specs = (
        P(None, "ctx"),
        P(),
        P("ctx", "head"),
        P(None, "ctx", None),
        P(None, "ctx", None),
        P("head", "ctx"),
        P(),
        P(),
    )
    out_specs = P("head", "ctx")
    return jax.shard_map(shards, mesh=mesh, in_specs=in_specs, out_specs=out_specs, check_vma=False)
```

profile of v0, /device:TPU:0, one launch (start us, length us, event | category | flops | bytes accessed | tf_op | source)
XLA Modules:
  0.0 222.7 jit_solution(15778530597544170264)
XLA Ops:
  6.5 0.0 copy-start
  6.5 0.0 reduce-scatter.3.cloned.1.call-start
  6.5 1.3 fusion.14
  7.9 23.1 %psum.7 = f32[256,1]{0,1:T(1,128)S(1)} all-reduce(f32[256,1]{0,1:T(1,128)S(1)} %bitcast.42), channel_id=1, replica_groups=mesh['ctx'=8,'head'=4] {'ctx'}, use_global_device_ids=true, to_apply=%region_1.0 | all-reduce | flops 256 | bytes 2048 | tf_op jit(solution)/shard_map/psum | solution.py:29
  31.0 0.7 dynamic_slice.2
  31.6 5.5 %fusion.19 = f32[256,2048]{0,1:T(8,128)} fusion(bf16[1024,2048]{1,0:T(8,128)(2,1)} %param.10, bf16[256,1024]{1,0:T(8,128)(2,1)} %param.8, f32[1024]{0:T(1024)S(1)} %dynamic_slice.2, f32[256]{0:T(256)S(1)} %bitcast.43), kind=kOutput, calls=%fused_computation.22 | convolution fusion | flops 1074790400 | bytes 6820864 | tf_op jit(solution)/shard_map/reshape | solution.py:34
  37.2 0.0 reduce-scatter.3.cloned.1.call-update
  37.2 0.0 copy-done
  37.2 0.7 gather_fusion.1
  38.0 2.0 gather_fusion
  40.0 0.0 copy-start.2
  40.0 0.0 copy-start.3
  40.0 1.5 pad_maximum_fusion
  41.5 3.6 %all-to-all-start = ((bf16[8,2,512,128]{3,2,1,0:T(8,128)(2,1)}), bf16[8,2,512,128]{3,2,1,0:T(8,128)(2,1)S(1)}, u32[]{:S(2)}, u32[]{:S(2)}) async-start(bf16[8,2,512,128]{3,2,1,0:T(8,128)(2,1)} %pad_maximum_fusion), calls=%async_computation.1 | async-start | bytes 4194304 | tf_op jit(solution)/shard_map/all_to_all | solution.py:40
  45.1 0.0 all-gather.2.cloned.1.call-start
  45.1 0.0 copy-done.2
  45.2 0.0 copy-done.3
  45.2 1.9 fusion.6
  47.0 59.5 %all-to-all-done = bf16[8,2,512,128]{3,2,1,0:T(8,128)(2,1)S(1)} async-done(((bf16[8,2,512,128]{3,2,1,0:T(8,128)(2,1)}), bf16[8,2,512,128]{3,2,1,0:T(8,128)(2,1)S(1)}, u32[]{:S(2)}, u32[]{:S(2)}) %all-to-all-start) | async-done | bytes 2097184 | tf_op jit(solution)/shard_map/all_to_all | solution.py:40
  106.5 1.5 fusion.29
  108.0 25.2 %reduce-scatter.3.cloned.1.call-done = f32[1,256,256]{1,2,0:T(8,128)} async-done(((f32[8,256,256]{1,2,0:T(8,128)}), f32[1,256,256]{1,2,0:T(8,128)}) %reduce-scatter.3.cloned.1.call-update) | async-done | bytes 262160 | tf_op jit(solution)/shard_map/reduce_scatter | solution.py:36
  133.2 1.0 convert_element_type.21
  134.2 0.0 copy-start.1
  134.2 8.3 %fusion.30 = (f32[256,2]{0,1:T(2,128)S(1)}, bf16[256,2,4096]{2,0,1:T(8,128)(2,1)}) fusion(pred[256,4096]{1,0:T(8,128)(4,1)} %fusion.6, bf16[256,2,128]{0,2,1:T(8,128)(2,1)S(1)} %bitcast.41, bf16[4096,128,1]{1,0,2:T(8,128)(2,1)} %bitcast.39), kind=kOutput, calls=%fused_computation.43 | convolution fusion | flops 549457920 | bytes 6424576 | tf_op jit(solution)/shard_map/sub | solution.py:55
  142.5 0.0 copy-done.1
  142.5 3.7 %fusion.11 = bf16[256,2,128]{0,2,1:T(8,128)(2,1)S(1)} fusion(bf16[4096,128,1]{1,0,2:T(8,128)(2,1)S(1)} %bitcast.34, bf16[256,2,4096]{2,0,1:T(8,128)(2,1)} %get-tuple-element.8, f32[256,2]{0,1:T(2,128)S(1)} %get-tuple-element.7), kind=kOutput, calls=%fused_computation.17 | convolution fusion | flops 537001984 | bytes 5376000 | tf_op jit(solution)/shard_map/nhj,jd->nhd/dot_general | solution.py:57
  146.2 0.8 copy.20
  146.9 0.0 all-gather.2.cloned.1.call-update
  147.0 0.0 reduce-scatter.5.cloned.1.call-start
  147.0 39.4 %all-gather.2.cloned.1.call-done = bf16[8,256,256]{2,1,0:T(8,128)(2,1)} async-done(((bf16[1,256,256]{2,1,0:T(8,128)(2,1)}), bf16[8,256,256]{2,1,0:T(8,128)(2,1)}) %all-gather.2.cloned.1.call-update) | async-done | bytes 1048592 | tf_op jit(solution)/shard_map/all_gather | solution.py:61
  186.4 1.5 copy.21
  187.9 4.5 %fusion.31 = f32[256,1024]{1,0:T(8,128)} fusion(bf16[256,2048]{0,1:T(8,128)(2,1)S(1)} %bitcast.38, bf16[2048,1024]{1,0:T(8,128)(2,1)} %param.13), kind=kOutput, calls=%fused_computation.44 | convolution fusion | flops 1073741824 | bytes 6291456 | tf_op jit(solution)/shard_map/dot_general | solution.py:65
  192.4 0.0 reduce-scatter.5.cloned.1.call-update
  192.4 23.8 %reduce-scatter.5.cloned.1.call-done = f32[64,1024]{1,0:T(8,128)} async-done(((f32[256,1024]{1,0:T(8,128)}), f32[64,1024]{1,0:T(8,128)}) %reduce-scatter.5.cloned.1.call-update) | async-done | bytes 262160 | tf_op jit(solution)/shard_map/reduce_scatter | solution.py:64
  (4 shorter events, 0.0 us)
Async XLA Ops:
  6.5 30.7 %copy-start = (bf16[8,512,128]{2,1,0:T(8,128)(2,1)S(1)}, bf16[8,512,128]{2,1,0:T(8,128)(2,1)}, u32[]{:S(2)}) copy-start(bf16[8,512,128]{2,1,0:T(8,128)(2,1)} %param.12) | copy-start | bytes 3145732
  6.5 126.7 %reduce-scatter.3.cloned.1.call-start = ((), (), s32[]{:S(2)}) async-start(), calls=%async_computation.3 | async-start | bytes 2359296 | tf_op jit(solution)/shard_map/reduce_scatter | solution.py:36
  40.0 5.2 %copy-start.2 = (s32[256]{0:T(256)S(1)}, s32[256]{0:T(256)}, u32[]{:S(2)}) copy-start(s32[256]{0:T(256)} %param.14) | copy-start | bytes 3076
  40.0 5.2 %copy-start.3 = (s32[256]{0:T(256)S(1)}, s32[256]{0:T(256)}, u32[]{:S(2)}) copy-start(s32[256]{0:T(256)} %param.15) | copy-start | bytes 3076
  41.5 65.0 %all-to-all-start = ((bf16[8,2,512,128]{3,2,1,0:T(8,128)(2,1)}), bf16[8,2,512,128]{3,2,1,0:T(8,128)(2,1)S(1)}, u32[]{:S(2)}, u32[]{:S(2)}) async-start(bf16[8,2,512,128]{3,2,1,0:T(8,128)(2,1)} %pad_maximum_fusion), calls=%async_computation.1 | async-start | bytes 4194304 | tf_op jit(solution)/shard_map/all_to_all | solution.py:40
  45.1 141.3 %all-gather.2.cloned.1.call-start = ((), (), s32[]{:S(2)}) async-start(), calls=%async_computation.4 | async-start | bytes 1179648 | tf_op jit(solution)/shard_map/all_gather | solution.py:61
  134.2 8.3 %copy-start.1 = (bf16[1,8,512,128]{3,2,0,1:T(8,128)(2,1)S(1)}, bf16[1,8,512,128]{3,2,0,1:T(8,128)(2,1)}, u32[]{:S(2)}) copy-start(bf16[1,8,512,128]{3,2,0,1:T(8,128)(2,1)} %get-tuple-element.6) | copy-start | bytes 3145732
  147.0 69.2 %reduce-scatter.5.cloned.1.call-start = ((), (), s32[]{:S(2)}) async-start(), calls=%async_computation.5 | async-start | bytes 1310720 | tf_op jit(solution)/shard_map/reduce_scatter | solution.py:64
Sparse Core Ops, SparseCore 0:
  37.3 95.8 reduce-scatter.2
  147.1 39.2 all-gather.1
  192.5 23.6 reduce-scatter.4
where the time goes:
time: 223 us
  waiting for transfers between devices  148 us (66%)
  blocking collectives  23.1 us (10%)
  matrix products  22 us (10%)
  between operations  13.2 us (6%)
  local copies, waits for them, and re-layouts  7.19 us (3%)
  other arithmetic  5.66 us (3%)
  starting transfers between devices  3.69 us (2%)
    all_to_all x1, waiting for transfers between devices, shards(): kv = lax.all_to_all(kv, 'ctx', split_axis=0, concat_axis=0, tiled=True)  59.5 us
    all_gather x1, waiting for transfers between devices, shards(): attn = lax.all_gather(attn, 'ctx', axis=0, tiled=False)  39.4 us
    reduce_scatter x1, waiting for transfers between devices, shards(): lax.psum_scatter(partial, 'ctx', scatter_dimension=0, tiled=False)  25.2 us
    reduce_scatter x1, waiting for transfers between devices, shards(): lax.psum_scatter(jnp.dot(attn, w_output, preferred_element_type=jnp.float...  23.8 us
    psum x1, blocking collectives, shards(): lax.psum(jnp.sum(widened * widened, axis=1, keepdims=True), 'ctx')  23.1 us
    sub x1, matrix products, shards(): expo = jnp.where(usable, jnp.exp(scores - row_max), 0.0)  8.3 us
    reshape x1, matrix products, shards(): partial.reshape(rsplit, rows_dev, hsplit, heads_dev * HD)  5.51 us
    dot_general x1, matrix products, shards(): jnp.dot(attn, w_output, preferred_element_type=jnp.float32)  4.46 us
  transfers between devices with their start and end apart: 4, of which 4 were waited for; matrix products, arithmetic and copies ran while one was open for 3% of the time, Pallas kernels for 0%

commit v1 on v0

--- a/solution.py
+++ b/solution.py
@@ -26,7 +26,9 @@
     rows_dev = rows // rsplit
     heads_dev = heads_here // hsplit
     widened = hidden.astype(jnp.float32)
-    total_sq = lax.psum(jnp.sum(widened * widened, axis=1, keepdims=True), "ctx")
+    own = jnp.sum(widened * widened, axis=1, keepdims=True)
+    pieces = lax.all_gather(own, "ctx", axis=0, tiled=False)
+    total_sq = pieces.sum(axis=0)
     inv_rms = lax.rsqrt(total_sq / d_model + 1e-05)
     gain = lax.dynamic_slice_in_dim(norm_gain, ctx_index * feat, feat, 0)
     normed = (widened * inv_rms * gain[None, :]).astype(jnp.bfloat16)

time: 223 us -> 222 us (level)
    psum x1 -> x0, blocking collectives: 23.1 us -> none  [shards(): lax.psum(jnp.sum(widened * widened, axis=1, keepdims=True), 'ctx')]
    all_gather x0 -> x1, blocking collectives: none -> 22.2 us  [shards(): pieces = lax.all_gather(own, 'ctx', axis=0, tiled=False)]
where the time goes in v1:
time: 222 us
  waiting for transfers between devices  148 us (67%)
  blocking collectives  22.2 us (10%)
  matrix products  22 us (10%)
  between operations  13.2 us (6%)
  local copies, waits for them, and re-layouts  7.18 us (3%)
  other arithmetic  5.69 us (3%)
  starting transfers between devices  3.69 us (2%)
    all_to_all x1, waiting for transfers between devices, shards(): kv = lax.all_to_all(kv, 'ctx', split_axis=0, concat_axis=0, tiled=True)  59.5 us
    all_gather x1, waiting for transfers between devices, shards(): attn = lax.all_gather(attn, 'ctx', axis=0, tiled=False)  39.4 us
    reduce_scatter x1, waiting for transfers between devices, shards(): lax.psum_scatter(partial, 'ctx', scatter_dimension=0, tiled=False)  25.2 us
    reduce_scatter x1, waiting for transfers between devices, shards(): lax.psum_scatter(jnp.dot(attn, w_output, preferred_element_type=jnp.float...  23.8 us
    all_gather x1, blocking collectives, shards(): pieces = lax.all_gather(own, 'ctx', axis=0, tiled=False)  22.2 us
    sub x1, matrix products, shards(): expo = jnp.where(usable, jnp.exp(scores - row_max), 0.0)  8.3 us
    reshape x1, matrix products, shards(): partial.reshape(rsplit, rows_dev, hsplit, heads_dev * HD)  5.51 us
    dot_general x1, matrix products, shards(): jnp.dot(attn, w_output, preferred_element_type=jnp.float32)  4.46 us
  transfers between devices with their start and end apart: 4, of which 4 were waited for; matrix products, arithmetic and copies ran while one was open for 3% of the time, Pallas kernels for 0%

profile of v1, /device:TPU:0, one launch (start us, length us, event | category | flops | bytes accessed | tf_op | source)
XLA Modules:
  0.0 221.9 jit_solution(16769434317280432649)
XLA Ops:
  6.5 0.0 copy-start
  6.5 0.0 reduce-scatter.3.cloned.1.call-start
  6.5 1.3 fusion.14
  7.9 22.2 %all-gather.1 = f32[8,1,256]{2,1,0:T(1,128)S(1)} all-gather(f32[1,1,256]{2,1,0:T(1,128)S(1)} %bitcast.41), channel_id=2, replica_groups=mesh['ctx'=8,'head'=4] {'ctx'}, dimensions={0}, use_global_device_ids=true | all-gather | bytes 9216 | tf_op jit(solution)/shard_map/all_gather | solution.py:30
  30.1 0.7 dynamic_slice.2
  30.8 5.5 %fusion.19 = f32[256,2048]{0,1:T(8,128)} fusion(bf16[1024,2048]{1,0:T(8,128)(2,1)} %param.10, bf16[256,1024]{1,0:T(8,128)(2,1)} %param.8, f32[1024]{0:T(1024)S(1)} %dynamic_slice.2, f32[256]{0:T(256)S(1)} %add_rsqrt_fusion), kind=kOutput, calls=%fused_computation.22 | convolution fusion | flops 1074790400 | bytes 6820864 | tf_op jit(solution)/shard_map/reshape | solution.py:36
  36.3 0.0 reduce-scatter.3.cloned.1.call-update
  36.4 0.0 copy-done
  36.4 0.7 gather_fusion.1
  37.2 2.0 gather_fusion
  39.1 0.0 copy-start.2
  39.1 0.0 copy-start.3
  39.2 1.5 pad_maximum_fusion
  40.6 3.6 %all-to-all-start = ((bf16[8,2,512,128]{3,2,1,0:T(8,128)(2,1)}), bf16[8,2,512,128]{3,2,1,0:T(8,128)(2,1)S(1)}, u32[]{:S(2)}, u32[]{:S(2)}) async-start(bf16[8,2,512,128]{3,2,1,0:T(8,128)(2,1)} %pad_maximum_fusion), calls=%async_computation.1 | async-start | bytes 4194304 | tf_op jit(solution)/shard_map/all_to_all | solution.py:42
  44.2 0.0 all-gather.4.cloned.1.call-start
  44.3 0.0 copy-done.2
  44.3 0.0 copy-done.3
  44.3 1.9 fusion.6
  46.2 59.5 %all-to-all-done = bf16[8,2,512,128]{3,2,1,0:T(8,128)(2,1)S(1)} async-done(((bf16[8,2,512,128]{3,2,1,0:T(8,128)(2,1)}), bf16[8,2,512,128]{3,2,1,0:T(8,128)(2,1)S(1)}, u32[]{:S(2)}, u32[]{:S(2)}) %all-to-all-start) | async-done | bytes 2097184 | tf_op jit(solution)/shard_map/all_to_all | solution.py:42
  105.7 1.5 fusion.29
  107.2 25.2 %reduce-scatter.3.cloned.1.call-done = f32[1,256,256]{1,2,0:T(8,128)} async-done(((f32[8,256,256]{1,2,0:T(8,128)}), f32[1,256,256]{1,2,0:T(8,128)}) %reduce-scatter.3.cloned.1.call-update) | async-done | bytes 262160 | tf_op jit(solution)/shard_map/reduce_scatter | solution.py:38
  132.4 1.0 convert_element_type.21
  133.4 0.0 copy-start.1
  133.4 8.3 %fusion.30 = (f32[256,2]{0,1:T(2,128)S(1)}, bf16[256,2,4096]{2,0,1:T(8,128)(2,1)}) fusion(pred[256,4096]{1,0:T(8,128)(4,1)} %fusion.6, bf16[256,2,128]{0,2,1:T(8,128)(2,1)S(1)} %bitcast.40, bf16[4096,128,1]{1,0,2:T(8,128)(2,1)} %bitcast.38), kind=kOutput, calls=%fused_computation.43 | convolution fusion | flops 549457920 | bytes 6424576 | tf_op jit(solution)/shard_map/sub | solution.py:57
  141.7 0.0 copy-done.1
  141.7 3.7 %fusion.11 = bf16[256,2,128]{0,2,1:T(8,128)(2,1)S(1)} fusion(bf16[4096,128,1]{1,0,2:T(8,128)(2,1)S(1)} %bitcast.33, bf16[256,2,4096]{2,0,1:T(8,128)(2,1)} %get-tuple-element.8, f32[256,2]{0,1:T(2,128)S(1)} %get-tuple-element.7), kind=kOutput, calls=%fused_computation.17 | convolution fusion | flops 537001984 | bytes 5376000 | tf_op jit(solution)/shard_map/nhj,jd->nhd/dot_general | solution.py:59
  145.4 0.8 copy.20
  146.2 0.0 all-gather.4.cloned.1.call-update
  146.2 0.0 reduce-scatter.5.cloned.1.call-start
  146.2 39.4 %all-gather.4.cloned.1.call-done = bf16[8,256,256]{2,1,0:T(8,128)(2,1)} async-done(((bf16[1,256,256]{2,1,0:T(8,128)(2,1)}), bf16[8,256,256]{2,1,0:T(8,128)(2,1)}) %all-gather.4.cloned.1.call-update) | async-done | bytes 1048592 | tf_op jit(solution)/shard_map/all_gather | solution.py:63
  185.6 1.5 copy.21
  187.1 4.5 %fusion.31 = f32[256,1024]{1,0:T(8,128)} fusion(bf16[256,2048]{0,1:T(8,128)(2,1)S(1)} %bitcast.37, bf16[2048,1024]{1,0:T(8,128)(2,1)} %param.13), kind=kOutput, calls=%fused_computation.44 | convolution fusion | flops 1073741824 | bytes 6291456 | tf_op jit(solution)/shard_map/dot_general | solution.py:67
  191.5 0.0 reduce-scatter.5.cloned.1.call-update
  191.6 23.8 %reduce-scatter.5.cloned.1.call-done = f32[64,1024]{1,0:T(8,128)} async-done(((f32[256,1024]{1,0:T(8,128)}), f32[64,1024]{1,0:T(8,128)}) %reduce-scatter.5.cloned.1.call-update) | async-done | bytes 262160 | tf_op jit(solution)/shard_map/reduce_scatter | solution.py:66
  (5 shorter events, 0.1 us)
Async XLA Ops:
  6.5 29.9 %copy-start = (bf16[8,512,128]{2,1,0:T(8,128)(2,1)S(1)}, bf16[8,512,128]{2,1,0:T(8,128)(2,1)}, u32[]{:S(2)}) copy-start(bf16[8,512,128]{2,1,0:T(8,128)(2,1)} %param.12) | copy-start | bytes 3145732
  6.5 125.9 %reduce-scatter.3.cloned.1.call-start = ((), (), s32[]{:S(2)}) async-start(), calls=%async_computation.3 | async-start | bytes 2359296 | tf_op jit(solution)/shard_map/reduce_scatter | solution.py:38
  39.1 5.2 %copy-start.2 = (s32[256]{0:T(256)S(1)}, s32[256]{0:T(256)}, u32[]{:S(2)}) copy-start(s32[256]{0:T(256)} %param.14) | copy-start | bytes 3076
  39.1 5.2 %copy-start.3 = (s32[256]{0:T(256)S(1)}, s32[256]{0:T(256)}, u32[]{:S(2)}) copy-start(s32[256]{0:T(256)} %param.15) | copy-start | bytes 3076
  40.6 65.0 %all-to-all-start = ((bf16[8,2,512,128]{3,2,1,0:T(8,128)(2,1)}), bf16[8,2,512,128]{3,2,1,0:T(8,128)(2,1)S(1)}, u32[]{:S(2)}, u32[]{:S(2)}) async-start(bf16[8,2,512,128]{3,2,1,0:T(8,128)(2,1)} %pad_maximum_fusion), calls=%async_computation.1 | async-start | bytes 4194304 | tf_op jit(solution)/shard_map/all_to_all | solution.py:42
  44.2 141.3 %all-gather.4.cloned.1.call-start = ((), (), s32[]{:S(2)}) async-start(), calls=%async_computation.4 | async-start | bytes 1179648 | tf_op jit(solution)/shard_map/all_gather | solution.py:63
  133.4 8.3 %copy-start.1 = (bf16[1,8,512,128]{3,2,0,1:T(8,128)(2,1)S(1)}, bf16[1,8,512,128]{3,2,0,1:T(8,128)(2,1)}, u32[]{:S(2)}) copy-start(bf16[1,8,512,128]{3,2,0,1:T(8,128)(2,1)} %get-tuple-element.6) | copy-start | bytes 3145732
  146.2 69.2 %reduce-scatter.5.cloned.1.call-start = ((), (), s32[]{:S(2)}) async-start(), calls=%async_computation.5 | async-start | bytes 1310720 | tf_op jit(solution)/shard_map/reduce_scatter | solution.py:66
Sparse Core Ops, SparseCore 0:
  36.5 95.8 reduce-scatter.2
  146.3 39.2 all-gather.3
  191.7 23.6 reduce-scatter.4
